TPU v7x, 256 devices: a whole 4x4x8 slice. The times are simulated.
256 devices in a mesh: seg: 64 (over y, z, core), ch: 4 (over x).
Axes of the slice: x: 4, y: 4, z: 8, core: 2. Of those that a mesh axis runs over, the one named last changes fastest.
Arguments:
- voxels: bfloat16 [65536, 256], P('seg'), may hold values from -6 to 6
- neighbours: int32 [27, 65536], P(None, 'seg'), may hold values from -1 to 65535, as said below
- send_perm: int32 [64, 1024], P('seg'), may hold values from 0 to 1023, each once within a row
- send_counts: int32 [64, 64], replicated, may hold values from 0 to 32, as said below
- conv_weight: bfloat16 [27, 256, 256], P(None, None, 'ch'), may hold values from -0.078125 to 0.078125
- qkv_first: bfloat16 [256, 3, 256], P(None, None, 'ch'), may hold values from -3 to 3
- out_first: bfloat16 [256, 256], replicated, may hold values from -0.375 to 0.375
- qkv_second: bfloat16 [256, 3, 256], P(None, None, 'ch'), may hold values from -3 to 3
- out_second: bfloat16 [256, 256], replicated, may hold values from -0.375 to 0.375
Outputs:
- encoded: bfloat16 [65536, 256], P('seg', 'ch')
Inputs may be any that keep to these rules, and one draw needn't show every extreme that they name: `neighbours`: -1 marks an absent neighbour; any other entry is a voxel within 128 positions of the entry's own voxel along the z-order curve, and the middle offset is the voxel itself. `send_counts`: each row sums to 1024; some Hilbert segment receives exactly 32 voxels from every z-order segment.
All inputs are finite; a program needn't handle non-finite values.
Results may differ from a plain program's by a relative error of at most 0.02.
Values may be sent and summed in bfloat16 or wider, within the bound.
No kernel may reach another device: no remote copies, remote signals or barrier semaphores. Data moves between devices by JAX's collectives and lax.ppermute only.
A program may use at most 64 MiB of HBM per device.

v0:
```python
import jax
import jax.numpy as jnp
from jax import lax
from jax.sharding import PartitionSpec as P

HD = 16
PATCH = 1024
KOFF = 27
HALO = 128
NORM_EPS = 1e-05
MASKED_SCORE = -1e30


def extended(cells, sides, width):
    for axis, dim in sides:
        count = lax.axis_size(axis)
        ends = count - 1
        head = lax.slice_in_dim(cells, 0, width, axis=dim)
        tail = lax.slice_in_dim(cells, cells.shape[dim] - width, cells.shape[dim], axis=dim)
        cells = jnp.concatenate(
            [
                lax.ppermute(tail, axis, [(i, (i + 1) % count) for i in range(ends)]),
                cells,
                lax.ppermute(head, axis, [((i + 1) % count, i) for i in range(ends)]),
            ],
            axis=dim,
        )
    return cells


def layer_norm(rows_in):
    values32 = rows_in.astype(jnp.float32)
    centre = values32 - jnp.mean(values32, axis=-1, keepdims=True)
    spread = jnp.mean(centre * centre, axis=-1, keepdims=True)
    return (centre * lax.rsqrt(spread + NORM_EPS)).astype(jnp.bfloat16)


def project(normed, weight):
    width_in, stacked, local_cols = weight.shape
    product = jnp.dot(
        normed, weight.reshape(width_in, stacked * local_cols), preferred_element_type=jnp.float32
    )
    return product.astype(jnp.bfloat16).reshape(normed.shape[0], stacked, local_cols // HD, HD)


def patch_attention(qkv_rows, key_live):
    count_rows, stacked, head_count, head_dim = qkv_rows.shape
    query_rows = min(512, PATCH)
    score_scale = head_dim ** (-0.5)
    grouped = qkv_rows.reshape(count_rows // PATCH, PATCH, stacked, head_count, head_dim)
    masks = key_live.reshape(count_rows // PATCH, PATCH)

    def one_patch(packed_item):
        patch_rows, live_keys = packed_item
        key_rows = patch_rows[:, 1]
        value_rows = patch_rows[:, 2]
        query_blocks = patch_rows[:, 0].reshape(
            PATCH // query_rows, query_rows, head_count, head_dim
        )

        def one_block(query_block):
            scores = (
                jnp.einsum(
                    "qhd,khd->hqk", query_block, key_rows, preferred_element_type=jnp.float32
                )
                * score_scale
            )
            scores = jnp.where(live_keys[None, None, :], scores, MASKED_SCORE)
            peak = jnp.max(scores, axis=2, keepdims=True)
            powered = jnp.exp(scores - peak)
            normaliser = jnp.sum(powered, axis=2)
            blended = jnp.einsum(
                "hqk,khd->qhd",
                powered.astype(jnp.bfloat16),
                value_rows,
                preferred_element_type=jnp.float32,
            )
            return (blended / jnp.transpose(normaliser)[:, :, None]).astype(jnp.bfloat16)

        return lax.map(one_block, query_blocks).reshape(PATCH, head_count * head_dim)

    return lax.map(one_patch, (grouped, masks)).reshape(count_rows, head_count * head_dim)


def local(
    voxels,
    neighbours,
    send_perm,
    send_counts,
    conv_weight,
    qkv_first,
    out_first,
    qkv_second,
    out_second,
):
    seg_index = lax.axis_index("seg")
    seg_count = lax.axis_size("seg")
    ch_index = lax.axis_index("ch")
    rows_dev, channels = voxels.shape
    quarter = conv_weight.shape[2]
    bucket_rows = 2 * rows_dev // seg_count
    total_slots = seg_count * bucket_rows
    padded = extended(voxels, (("seg", 0),), HALO)
    first_row = seg_index * rows_dev - HALO
    padded_rows = rows_dev + 2 * HALO

    def conv_step(kernel_index, running):
        target = neighbours[kernel_index]
        local_row = jnp.clip(target - first_row, 0, padded_rows - 1)
        picked = jnp.take(padded, local_row, axis=0)
        picked = jnp.where((target >= 0)[:, None], picked, jnp.zeros((), jnp.bfloat16))
        return running + jnp.dot(
            picked, conv_weight[kernel_index], preferred_element_type=jnp.float32
        )

    conv_sum = lax.fori_loop(0, KOFF, conv_step, jnp.zeros((rows_dev, quarter), jnp.float32))
    own_cols = lax.dynamic_slice_in_dim(voxels, ch_index * quarter, quarter, 1)
    mixed_a_part = (own_cols.astype(jnp.float32) + conv_sum).astype(jnp.bfloat16)
    mixed_a = lax.all_gather(mixed_a_part, "ch", axis=1, tiled=True)
    qkv_a = project(layer_norm(mixed_a), qkv_first)
    heads_a = patch_attention(qkv_a, jnp.ones((rows_dev,), bool))
    out_rows = lax.dynamic_slice_in_dim(out_first, ch_index * quarter, quarter, 0)
    partial_one = jnp.dot(heads_a, out_rows, preferred_element_type=jnp.float32)
    attn_one = lax.psum(partial_one.astype(jnp.bfloat16), "ch").astype(jnp.float32)
    mixed_b = (mixed_a.astype(jnp.float32) + attn_one).astype(jnp.bfloat16)
    mixed_b_part = lax.dynamic_slice_in_dim(mixed_b, ch_index * quarter, quarter, 1)
    counts_row = lax.dynamic_index_in_dim(send_counts, seg_index, 0, keepdims=False)
    send_off = jnp.cumsum(counts_row) - counts_row
    send_end = send_off + counts_row
    send_order = send_perm[0]
    bucket_pos = send_off[:, None] + jnp.arange(bucket_rows, dtype=jnp.int32)[None, :]
    send_rows = send_order[jnp.clip(bucket_pos, 0, rows_dev - 1)].reshape(-1)
    counts_col = lax.dynamic_index_in_dim(send_counts, seg_index, 1, keepdims=False)
    recv_off = jnp.cumsum(counts_col) - counts_col
    recv_end = recv_off + counts_col
    slots = jnp.arange(total_slots, dtype=jnp.int32)
    source = jnp.minimum(
        jnp.sum((recv_end[None, :] <= slots[:, None]).astype(jnp.int32), axis=1), seg_count - 1
    )
    within = jnp.clip(slots - recv_off[source], 0, bucket_rows - 1)
    flat_from = source * bucket_rows + within
    live_keys = slots < jnp.sum(counts_col)
    qkv_b = project(layer_norm(mixed_b), qkv_second)
    head_local = qkv_b.shape[2]
    outgoing = jnp.take(qkv_b.reshape(rows_dev, 3 * quarter), send_rows, axis=0).reshape(
        seg_count, bucket_rows, 3 * quarter
    )
    arrived = lax.all_to_all(outgoing, "seg", split_axis=0, concat_axis=0, tiled=True).reshape(
        total_slots, 3 * quarter
    )
    compact = jnp.take(arrived, flat_from, axis=0).reshape(total_slots, 3, head_local, HD)
    heads_owner = patch_attention(compact, live_keys)
    bucket_from = jnp.clip(
        recv_off[:, None] + jnp.arange(bucket_rows, dtype=jnp.int32)[None, :], 0, total_slots - 1
    ).reshape(-1)
    going_home = jnp.take(heads_owner, bucket_from, axis=0).reshape(seg_count, bucket_rows, quarter)
    returned = lax.all_to_all(going_home, "seg", split_axis=0, concat_axis=0, tiled=True).reshape(
        total_slots, quarter
    )
    inverse = (
        jnp.zeros((rows_dev,), jnp.int32).at[send_order].set(jnp.arange(rows_dev, dtype=jnp.int32))
    )
    owner_of = jnp.minimum(
        jnp.sum((send_end[None, :] <= inverse[:, None]).astype(jnp.int32), axis=1), seg_count - 1
    )
    home_from = owner_of * bucket_rows + jnp.clip(inverse - send_off[owner_of], 0, bucket_rows - 1)
    heads_b = jnp.take(returned, home_from, axis=0)
    out_rows_two = lax.dynamic_slice_in_dim(out_second, ch_index * quarter, quarter, 0)
    partial_two = jnp.dot(heads_b, out_rows_two, preferred_element_type=jnp.float32)
    attn_two = lax.psum_scatter(
        partial_two.astype(jnp.bfloat16), "ch", scatter_dimension=1, tiled=True
    ).astype(jnp.float32)
    return (mixed_b_part.astype(jnp.float32) + attn_two).astype(jnp.bfloat16)


def solution(mesh):
    placed = (
        P("seg", None),
        P(None, "seg"),
        P("seg", None),
        P(),
        P(None, None, "ch"),
        P(None, None, "ch"),
        P(),
        P(None, None, "ch"),
        P(),
    )
    return jax.shard_map(
        local, mesh=mesh, in_specs=placed, out_specs=P("seg", "ch"), check_vma=False
    )
```

profile of v0, /device:TPU:8, one launch (start us, length us, event | category | flops | bytes accessed | tf_op | source)
XLA Modules:
  0.0 519.8 jit_solution(14209222011439790130)
XLA Ops:
  7.5 7.1 %collective-permute-start.1 = (bf16[128,256]{1,0:T(8,128)(2,1)S(1)}, bf16[128,256]{1,0:T(8,128)(2,1)S(1)}, u32[]{:S(2)}, u32[]{:S(2)}) collective-permute-start(bf16[128,256]{1,0:T(8,128)(2,1)S(1)} %get-tuple-element.486), channel_id=1, source_target_pairs={{4,0},{8,4},{12,8},{16,12},{20,16},{24,20},{28,24},{32,28},{36,32}... | collective-permute-start | bytes 196616 | tf_op jit(solution)/shard_map/ppermute | solution.py:24
  28.0 8.6 %gather_fusion.1 = s32[2048]{0:T(1024)S(1)} fusion(s32[1024]{0:T(1024)S(1)} %bitcast.276, s32[2048]{0:T(1024)S(1)} %broadcast_clamp_fusion.4), kind=kCustom, calls=%fused_computation.1 | custom fusion | bytes 24576 | tf_op jit(solution)/shard_map/gather | solution.py:132
  36.7 4.4 compare_select_fusion.9
  42.6 35.6 %select_select_fusion = s32[2048]{0:T(1024)S(1)} fusion(pred[2048]{0:T(1024)(128)(4,1)S(1)} %get-tuple-element.368, pred[2048]{0:T(1024)(128)(4,1)S(1)} %get-tuple-element.367, pred[2048]{0:T(1024)(128)(4,1)S(1)} %get-tuple-element.366, pred[2048]{0:T(1024)(128)(4,1)S(1)} %get-tuple-element.365, pred[2048]{0:T(1024)(128)(4,1)S(1)} %get-tuple-element.364, ...), kind=kLoop, calls=%fused_computation.244 | loop fusion | flops 116736 | bytes 133348 | tf_op jit(solution)/shard_map/gather | solution.py:140
  78.4 4.3 scatter_custom_fusion
  82.8 4.9 compare_select_fusion.18
  90.1 184.9 %while.55 = (s32[]{:T(128)}, f32[1024,64]{0,1:T(8,128)S(1)}, s32[27,1024]{1,0:T(8,128)}, s32[]{:T(128)}, bf16[1280,256]{1,0:T(8,128)(2,1)S(1)}, /*index=5*/bf16[27,256,64]{1,2,0:T(8,128)(2,1)}, s32[]{:T(128)}, s32[]{:T(128)}) while((s32[]{:T(128)}, f32[1024,64]{0,1:T(8,128)S(1)}, s32[27,1024]{1,0:T(8,128)}, s32[]{:T(128)}, ...), condition=%wide.region_1.2_spmd.clone, body=%wide.region_0.1_spmd.clone.sunk | while | flops 34223104 | bytes 2166903 | solution.py:116
  90.9 3.9 gather_fusion
  97.7 3.9 gather_fusion
  104.6 3.9 gather_fusion
  111.4 3.9 gather_fusion
  118.3 3.9 gather_fusion
  125.1 3.9 gather_fusion
  132.0 3.9 gather_fusion
  138.8 3.9 gather_fusion
  145.7 3.9 gather_fusion
  152.5 3.9 gather_fusion
  159.4 3.9 gather_fusion
  275.0 13.3 %all_gather.3 = bf16[1024,256]{0,1:T(8,128)(2,1)S(1)} all-gather(bf16[1024,64]{0,1:T(8,128)(2,1)S(1)} %add_convert_fusion.1), channel_id=1, replica_groups=mesh['seg'=64,'ch'=4] {'ch'}, dimensions={1}, use_global_device_ids=true | all-gather | bytes 655360 | tf_op jit(solution)/shard_map/all_gather | solution.py:119
  289.0 9.8 %while.52 = (s32[]{:T(128)}, bf16[2,512,4,16]{1,3,2,0:T(8,128)(2,1)S(1)}, bf16[2,512,4,16]{1,3,2,0:T(8,128)(2,1)S(1)}, bf16[1024,4,16]{0,2,1:T(8,128)(2,1)S(1)}, bf16[1024,4,16]{0,2,1:T(8,128)(2,1)S(1)}, /*index=5*/s32[]{:T(128)}) while((s32[]{:T(128)}, bf16[2,512,4,16]{1,3,2,0:T(8,128)(2,1)S(1)}, bf16[2,512,4,16]{1,3,2,0:T(8,128)(2,1)S(1)}, ...), condition=%wide.region_7.8_spmd, body=%wide.region_4.7_spmd.sunk | while | flops 151056384 | bytes 25600084 | solution.py:80
  301.0 45.8 %all-reduce.2.cloned.1.call-done = bf16[1024,256]{0,1:T(8,128)(2,1)} async-done(((bf16[1024,256]{0,1:T(8,128)(2,1)}), bf16[1024,256]{0,1:T(8,128)(2,1)}) %all-reduce.2.cloned.1.call-update) | async-done | bytes 524304 | tf_op jit(solution)/shard_map/psum | solution.py:124
  349.4 7.5 %gather_fusion.2 = bf16[2048,192]{1,0:T(8,128)(2,1)S(1)} fusion(bf16[1024,192]{1,0:T(8,128)(2,1)S(1)} %copy.62, s32[2048]{0:T(1024)S(1)} %broadcast_clamp_fusion.3), kind=kCustom, calls=%fused_computation.2 | custom fusion | bytes 1581056 | tf_op jit(solution)/shard_map/jit(_take)/gather | solution.py:145
  358.1 10.6 %all-to-all-start = ((bf16[64,32,192]{2,1,0:T(8,128)(2,1)}), bf16[64,32,192]{2,1,0:T(8,128)(2,1)S(1)}, u32[]{:S(2)}, u32[]{:S(2)}) async-start(bf16[64,32,192]{2,1,0:T(8,128)(2,1)} %broadcast_select_fusion.1), calls=%async_computation | async-start | bytes 2097152 | tf_op jit(solution)/shard_map/all_to_all | solution.py:148
  369.4 26.2 %all-to-all-done = bf16[64,32,192]{2,1,0:T(8,128)(2,1)S(1)} async-done(((bf16[64,32,192]{2,1,0:T(8,128)(2,1)}), bf16[64,32,192]{2,1,0:T(8,128)(2,1)S(1)}, u32[]{:S(2)}, u32[]{:S(2)}) %all-to-all-start) | async-done | bytes 786464 | tf_op jit(solution)/shard_map/all_to_all | solution.py:148
  395.6 7.5 %gather_fusion.3 = bf16[2048,192]{1,0:T(8,128)(2,1)S(1)} fusion(bf16[2048,192]{1,0:T(8,128)(2,1)S(1)} %bitcast.277, s32[2048]{0:T(1024)S(1)} %broadcast_clamp_fusion.2), kind=kCustom, calls=%fused_computation.3 | custom fusion | bytes 1581056 | tf_op jit(solution)/shard_map/jit(_take)/gather | solution.py:151
  405.5 22.2 %while.54 = (s32[]{:T(128)}, bf16[2,1024,64]{1,2,0:T(8,128)(2,1)S(1)}, bf16[2,1024,3,4,16]{1,4,3,2,0:T(8,128)(2,1)S(1)}, pred[2,1024]{1,0:T(4,128)(4,1)S(1)}, s32[]{:T(128)}, /*index=5*/s32[]{:T(128)}, s32[]{:T(128)}) while((s32[]{:T(128)}, bf16[2,1024,64]{1,2,0:T(8,128)(2,1)S(1)}, bf16[2,1024,3,4,16]{1,4,3,2,0:T(8,128)(2,1)S(1)}, ...), condition=%wide.region_22.23_spmd, body=%wide.region_17.22_spmd.sunk | while | flops 157347840 | bytes 28488956 | solution.py:82
  405.8 10.6 %while.56 = (s32[]{:T(128)}, bf16[2,512,4,16]{1,3,2,0:T(8,128)(2,1)S(1)}, pred[1024]{0:T(1024)(128)(4,1)S(1)}, bf16[2,512,4,16]{1,3,2,0:T(8,128)(2,1)S(1)}, bf16...) while((s32[]{:T(128)}, bf16[2,512,4,16]{1,3,2,0:T(8,128)(2,1)S(1)}, ...), condition=%wide.region_21.21_spmd, body=%wide.region_18.20_spmd.sunk | while | flops 157347840 | bytes 25603164 | solution.py:80
  416.9 10.6 %while.56 = (s32[]{:T(128)}, bf16[2,512,4,16]{1,3,2,0:T(8,128)(2,1)S(1)}, pred[1024]{0:T(1024)(128)(4,1)S(1)}, bf16[2,512,4,16]{1,3,2,0:T(8,128)(2,1)S(1)}, bf16...) while((s32[]{:T(128)}, bf16[2,512,4,16]{1,3,2,0:T(8,128)(2,1)S(1)}, ...), condition=%wide.region_21.21_spmd, body=%wide.region_18.20_spmd.sunk | while | flops 157347840 | bytes 25603164 | solution.py:80
  428.1 6.2 %gather_fusion.4 = bf16[2048,64]{1,0:T(8,128)(2,1)S(1)} fusion(bf16[2048,64]{1,0:T(8,128)(2,1)S(1)} %bitcast.278, s32[2048]{0:T(1024)S(1)} %copy-done.11), kind=kCustom, calls=%fused_computation.4 | custom fusion | bytes 532480 | tf_op jit(solution)/shard_map/jit(_take)/gather | solution.py:156
  435.6 7.8 %all-to-all-start.1 = ((bf16[64,2,1024]{2,1,0:T(2,128)(2,1)}), bf16[64,2,1024]{2,1,0:T(2,128)(2,1)S(1)}, u32[]{:S(2)}, u32[]{:S(2)}) async-start(bf16[64,2,1024]{2,1,0:T(2,128)(2,1)} %reshape.1017), calls=%async_computation.1 | async-start | bytes 524288 | tf_op jit(solution)/shard_map/all_to_all | solution.py:157
  444.6 36.5 %compare_and_fusion.4 = (pred[1024]{0:T(1024)(128)(4,1)S(1)}, s32[1024]{0:T(1024)S(1)}) fusion(s32[1024]{0:T(1024)S(1)} %copy-done.7, pred[1024]{0:T(1024)(128)(4,1)} %get-tuple-element.425, pred[1024]{0:T(1024)(128)(4,1)} %get-tuple-element.424, pred[1024]{0:T(1024)(128)(4,1)} %get-tuple-element.423, pred[1024]{0:T(1024)(128)(4,1)} %get-tuple-element.422, ...), kind=kLoop, calls=%fused_computation.258 | loop fusion | flops 69632 | bytes 76004 | tf_op jit(solution)/shard_map/jit(_take)/and | solution.py:167
  486.7 24.6 %reduce-scatter.4.cloned.1.call-done = bf16[64,1024]{1,0:T(8,128)(2,1)} async-done(((bf16[256,1024]{1,0:T(8,128)(2,1)}), bf16[64,1024]{1,0:T(8,128)(2,1)}) %reduce-scatter.4.cloned.1.call-update) | async-done | bytes 131088
  (374 shorter events, 209.3 us)
Async XLA Ops:
  6.5 292.5 %copy-start = (bf16[256,256]{1,0:T(8,128)(2,1)S(1)}, bf16[256,256]{1,0:T(8,128)(2,1)}, u32[]{:S(2)}) copy-start(bf16[256,256]{1,0:T(8,128)(2,1)} %param.23) | copy-start | bytes 393220
  6.5 340.2 %all-reduce.2.cloned.1.call-start = ((), (), s32[]{:S(2)}) async-start(), calls=%async_computation.3 | async-start | bytes 1048576 | tf_op jit(solution)/shard_map/psum | solution.py:124
  7.5 82.5 %collective-permute-start.1 = (bf16[128,256]{1,0:T(8,128)(2,1)S(1)}, bf16[128,256]{1,0:T(8,128)(2,1)S(1)}, u32[]{:S(2)}, u32[]{:S(2)}) collective-permute-start(bf16[128,256]{1,0:T(8,128)(2,1)S(1)} %get-tuple-element.486), channel_id=1, source_target_pairs={{4,0},{8,4},{12,8},{16,12},{20,16},{24,20},{28,24},{32,28},{36,32}... | collective-permute-start | bytes 196616 | tf_op jit(solution)/shard_map/ppermute | solution.py:24
  14.6 75.4 %collective-permute-start = (bf16[128,256]{1,0:T(8,128)(2,1)S(1)}, bf16[128,256]{1,0:T(8,128)(2,1)S(1)}, u32[]{:S(2)}, u32[]{:S(2)}) collective-permute-start(bf16[128,256]{1,0:T(8,128)(2,1)S(1)} %get-tuple-element.485), channel_id=1, source_target_pairs={{0,4},{4,8},{8,12},{12,16},{16,20},{20,24},{24,28},{28,32},{32,36}... | collective-permute-start | bytes 196616 | tf_op jit(solution)/shard_map/ppermute | solution.py:22
  24.5 64.7 %copy-start.3 = (s32[64]{0:T(128)}, s32[64]{0:T(128)S(1)}, u32[]{:S(2)}) copy-start(s32[64]{0:T(128)S(1)} %bitcast_subtract_fusion) | copy-start | bytes 772
  28.0 62.0 %copy-start.5 = (bf16[1024,256]{1,0:T(8,128)(2,1)S(1)}, bf16[1024,256]{1,0:T(8,128)(2,1)}, u32[]{:S(2)}) copy-start(bf16[1024,256]{1,0:T(8,128)(2,1)} %param.17) | copy-start | bytes 1572868
  90.0 198.5 %copy-start.47 = (bf16[256,3,64]{0,2,1:T(8,128)(2,1)S(1)}, bf16[256,3,64]{0,2,1:T(8,128)(2,1)}, u32[]{:S(2)}) copy-start(bf16[256,3,64]{0,2,1:T(8,128)(2,1)} %param.22) | copy-start | bytes 294916
  289.0 59.8 %copy-start.48 = (bf16[256,3,64]{0,2,1:T(8,128)(2,1)S(1)}, bf16[256,3,64]{0,2,1:T(8,128)(2,1)}, u32[]{:S(2)}) copy-start(bf16[256,3,64]{0,2,1:T(8,128)(2,1)} %param.24) | copy-start | bytes 294916
  358.1 37.5 %all-to-all-start = ((bf16[64,32,192]{2,1,0:T(8,128)(2,1)}), bf16[64,32,192]{2,1,0:T(8,128)(2,1)S(1)}, u32[]{:S(2)}, u32[]{:S(2)}) async-start(bf16[64,32,192]{2,1,0:T(8,128)(2,1)} %broadcast_select_fusion.1), calls=%async_computation | async-start | bytes 2097152 | tf_op jit(solution)/shard_map/all_to_all | solution.py:148
  405.2 39.0 %copy-start.7 = (s32[1024]{0:T(1024)S(1)}, s32[1024]{0:T(1024)}, u32[]{:S(2)}) copy-start(s32[1024]{0:T(1024)} %copy-done.6) | copy-start | bytes 12292
  405.2 39.0 %copy-start.9 = (s32[1024]{0:T(1024)S(1)}, s32[1024]{0:T(1024)}, u32[]{:S(2)}) copy-start(s32[1024]{0:T(1024)} %copy-done.8) | copy-start | bytes 12292
  405.2 39.0 %copy-start.12 = (s32[1024,1]{0,1:T(1,128)S(1)}, s32[1024,1]{0,1:T(1,128)}, u32[]{:S(2)}) copy-start(s32[1024,1]{0,1:T(1,128)} %get-tuple-element.472) | copy-start | bytes 12292
  405.2 39.0 %copy-start.13 = (pred[1024]{0:T(1024)(128)(4,1)S(1)}, pred[1024]{0:T(1024)(128)(4,1)}, u32[]{:S(2)}) copy-start(pred[1024]{0:T(1024)(128)(4,1)} %get-tuple-element.369) | copy-start | bytes 3076
  405.2 39.0 %copy-start.14 = (pred[1024]{0:T(1024)(128)(4,1)S(1)}, pred[1024]{0:T(1024)(128)(4,1)}, u32[]{:S(2)}) copy-start(pred[1024]{0:T(1024)(128)(4,1)} %get-tuple-element.370) | copy-start | bytes 3076
  405.2 39.0 %copy-start.15 = (pred[1024]{0:T(1024)(128)(4,1)S(1)}, pred[1024]{0:T(1024)(128)(4,1)}, u32[]{:S(2)}) copy-start(pred[1024]{0:T(1024)(128)(4,1)} %get-tuple-element.371) | copy-start | bytes 3076
  405.2 39.0 %copy-start.16 = (pred[1024]{0:T(1024)(128)(4,1)S(1)}, pred[1024]{0:T(1024)(128)(4,1)}, u32[]{:S(2)}) copy-start(pred[1024]{0:T(1024)(128)(4,1)} %get-tuple-element.372) | copy-start | bytes 3076
  405.2 39.0 %copy-start.17 = (pred[1024]{0:T(1024)(128)(4,1)S(1)}, pred[1024]{0:T(1024)(128)(4,1)}, u32[]{:S(2)}) copy-start(pred[1024]{0:T(1024)(128)(4,1)} %get-tuple-element.373) | copy-start | bytes 3076
  405.2 39.0 %copy-start.18 = (pred[1024]{0:T(1024)(128)(4,1)S(1)}, pred[1024]{0:T(1024)(128)(4,1)}, u32[]{:S(2)}) copy-start(pred[1024]{0:T(1024)(128)(4,1)} %get-tuple-element.374) | copy-start | bytes 3076
  405.2 39.0 %copy-start.19 = (pred[1024]{0:T(1024)(128)(4,1)S(1)}, pred[1024]{0:T(1024)(128)(4,1)}, u32[]{:S(2)}) copy-start(pred[1024]{0:T(1024)(128)(4,1)} %get-tuple-element.375) | copy-start | bytes 3076
  405.3 39.0 %copy-start.20 = (pred[1024]{0:T(1024)(128)(4,1)S(1)}, pred[1024]{0:T(1024)(128)(4,1)}, u32[]{:S(2)}) copy-start(pred[1024]{0:T(1024)(128)(4,1)} %get-tuple-element.376) | copy-start | bytes 3076
  405.3 39.0 %copy-start.21 = (pred[1024]{0:T(1024)(128)(4,1)S(1)}, pred[1024]{0:T(1024)(128)(4,1)}, u32[]{:S(2)}) copy-start(pred[1024]{0:T(1024)(128)(4,1)} %get-tuple-element.377) | copy-start | bytes 3076
  405.3 39.0 %copy-start.22 = (pred[1024]{0:T(1024)(128)(4,1)S(1)}, pred[1024]{0:T(1024)(128)(4,1)}, u32[]{:S(2)}) copy-start(pred[1024]{0:T(1024)(128)(4,1)} %get-tuple-element.378) | copy-start | bytes 3076
  405.3 39.0 %copy-start.23 = (pred[1024]{0:T(1024)(128)(4,1)S(1)}, pred[1024]{0:T(1024)(128)(4,1)}, u32[]{:S(2)}) copy-start(pred[1024]{0:T(1024)(128)(4,1)} %get-tuple-element.379) | copy-start | bytes 3076
  405.3 39.0 %copy-start.24 = (pred[1024]{0:T(1024)(128)(4,1)S(1)}, pred[1024]{0:T(1024)(128)(4,1)}, u32[]{:S(2)}) copy-start(pred[1024]{0:T(1024)(128)(4,1)} %get-tuple-element.380) | copy-start | bytes 3076
  405.3 39.0 %copy-start.25 = (pred[1024]{0:T(1024)(128)(4,1)S(1)}, pred[1024]{0:T(1024)(128)(4,1)}, u32[]{:S(2)}) copy-start(pred[1024]{0:T(1024)(128)(4,1)} %get-tuple-element.381) | copy-start | bytes 3076
  405.3 39.0 %copy-start.26 = (pred[1024]{0:T(1024)(128)(4,1)S(1)}, pred[1024]{0:T(1024)(128)(4,1)}, u32[]{:S(2)}) copy-start(pred[1024]{0:T(1024)(128)(4,1)} %get-tuple-element.382) | copy-start | bytes 3076
  405.3 39.0 %copy-start.27 = (pred[1024]{0:T(1024)(128)(4,1)S(1)}, pred[1024]{0:T(1024)(128)(4,1)}, u32[]{:S(2)}) copy-start(pred[1024]{0:T(1024)(128)(4,1)} %get-tuple-element.383) | copy-start | bytes 3076
  405.3 39.0 %copy-start.28 = (pred[1024]{0:T(1024)(128)(4,1)S(1)}, pred[1024]{0:T(1024)(128)(4,1)}, u32[]{:S(2)}) copy-start(pred[1024]{0:T(1024)(128)(4,1)} %get-tuple-element.384) | copy-start | bytes 3076
  405.3 39.0 %copy-start.29 = (pred[1024]{0:T(1024)(128)(4,1)S(1)}, pred[1024]{0:T(1024)(128)(4,1)}, u32[]{:S(2)}) copy-start(pred[1024]{0:T(1024)(128)(4,1)} %get-tuple-element.385) | copy-start | bytes 3076
  405.4 39.0 %copy-start.30 = (pred[1024]{0:T(1024)(128)(4,1)S(1)}, pred[1024]{0:T(1024)(128)(4,1)}, u32[]{:S(2)}) copy-start(pred[1024]{0:T(1024)(128)(4,1)} %get-tuple-element.386) | copy-start | bytes 3076
  435.6 45.5 %all-to-all-start.1 = ((bf16[64,2,1024]{2,1,0:T(2,128)(2,1)}), bf16[64,2,1024]{2,1,0:T(2,128)(2,1)S(1)}, u32[]{:S(2)}, u32[]{:S(2)}) async-start(bf16[64,2,1024]{2,1,0:T(2,128)(2,1)} %reshape.1017), calls=%async_computation.1 | async-start | bytes 524288 | tf_op jit(solution)/shard_map/all_to_all | solution.py:157
  443.4 67.9 %reduce-scatter.4.cloned.1.call-start = ((), (), s32[]{:S(2)}) async-start(), calls=%async_computation.4 | async-start | bytes 655360
  (23 other events, 751.7 us)
Sparse Core Ops, SparseCore 0:
  300.3 46.3 all-reduce.1
  486.8 24.4 reduce-scatter.3
where the time goes:
time: 527 us; the launch traced here: 520 us
  local copies, waits for them, and re-layouts  158 us (30%)
  other arithmetic  150 us (28%)
  waiting for transfers between devices  96.7 us (18%)
  matrix products  57.5 us (11%)
  starting transfers between devices  27.4 us (5%)
  between operations  14.6 us (3%)
  blocking collectives  13.3 us (3%)
    gather x27, local copies, waits for them, and re-layouts, conv_step(): picked = jnp.take(padded, local_row, axis=0)  106 us
    psum x1, waiting for transfers between devices, local(): lax.psum(partial_one.astype(jnp.bfloat16), 'ch').astype(jnp.float32)  45.8 us
    gather x3, other arithmetic, local(): within = jnp.clip(slots - recv_off[source], 0, bucket_rows - 1)  41.5 us
    and x1, other arithmetic, local(): heads_b = jnp.take(returned, home_from, axis=0)  36.5 us
    dot_general x27, matrix products, conv_step(): jnp.dot(picked, conv_weight[kernel_index], preferred_element_type=jnp.flo...  34.4 us
    all_to_all x1, waiting for transfers between devices, local(): lax.all_to_all(outgoing, 'seg', split_axis=0, concat_axis=0, tiled=True)  26.2 us
    unnamed x3, waiting for transfers between devices  24.6 us
    ge x27, other arithmetic, conv_step(): target >= 0  21.3 us
  transfers between devices with their start and end apart: 6, of which 3 were waited for; matrix products, arithmetic and copies ran while one was open for 22% of the time, Pallas kernels for 0%

commit v1 on v0

--- a/solution.py
+++ b/solution.py
@@ -121,7 +121,9 @@
     heads_a = patch_attention(qkv_a, jnp.ones((rows_dev,), bool))
     out_rows = lax.dynamic_slice_in_dim(out_first, ch_index * quarter, quarter, 0)
     partial_one = jnp.dot(heads_a, out_rows, preferred_element_type=jnp.float32)
-    attn_one = lax.psum(partial_one.astype(jnp.bfloat16), "ch").astype(jnp.float32)
+    attn_one = (
+        lax.all_gather(partial_one.astype(jnp.bfloat16), "ch").sum(axis=0).astype(jnp.float32)
+    )
     mixed_b = (mixed_a.astype(jnp.float32) + attn_one).astype(jnp.bfloat16)
     mixed_b_part = lax.dynamic_slice_in_dim(mixed_b, ch_index * quarter, quarter, 1)
     counts_row = lax.dynamic_index_in_dim(send_counts, seg_index, 0, keepdims=False)

time: 527 us -> 481 us (0.913)
  waiting for transfers between devices: 96.7 us -> 51.1 us
    psum x1 -> x0, waiting for transfers between devices: 45.8 us -> none  [local(): lax.psum(partial_one.astype(jnp.bfloat16), 'ch').astype(jnp.float32)]
    reduce_scatter x0 -> x1, waiting for transfers between devices: none -> 24.8 us  [local(): lax.psum_scatter(partial_two.astype(jnp.bfloat16), 'ch', scatter_dimensio...]
    unnamed x3 -> x2, waiting for transfers between devices: 24.6 us -> 0.03 us
  transfers between devices with their start and end apart: 6 -> 6, of which waited for: 3 -> 2; matrix products, arithmetic and copies ran while one was open for 22% -> 24% of each run, Pallas kernels for 0% -> 0%
where the time goes in v1:
time: 481 us; the launch traced here: 474 us
  local copies, waits for them, and re-layouts  159 us (33%)
  other arithmetic  152 us (32%)
  matrix products  57.5 us (12%)
  waiting for transfers between devices  51.1 us (11%)
  starting transfers between devices  24.9 us (5%)
  between operations  14.6 us (3%)
  blocking collectives  13.1 us (3%)
    gather x27, local copies, waits for them, and re-layouts, conv_step(): picked = jnp.take(padded, local_row, axis=0)  106 us
    gather x3, other arithmetic, local(): within = jnp.clip(slots - recv_off[source], 0, bucket_rows - 1)  41.7 us
    and x1, other arithmetic, local(): heads_b = jnp.take(returned, home_from, axis=0)  36.5 us
    dot_general x27, matrix products, conv_step(): jnp.dot(picked, conv_weight[kernel_index], preferred_element_type=jnp.flo...  34.4 us
    all_to_all x1, waiting for transfers between devices, local(): lax.all_to_all(outgoing, 'seg', split_axis=0, concat_axis=0, tiled=True)  26.2 us
    reduce_scatter x1, waiting for transfers between devices, local(): lax.psum_scatter(partial_two.astype(jnp.bfloat16), 'ch', scatter_dimensio...  24.8 us
    ge x27, other arithmetic, conv_step(): target >= 0  21.3 us
    select_n x27, other arithmetic, conv_step(): picked = jnp.take(padded, local_row, axis=0)  21.1 us
  transfers between devices with their start and end apart: 6, of which 2 were waited for; matrix products, arithmetic and copies ran while one was open for 24% of the time, Pallas kernels for 0%

profile of v1, /device:TPU:8, one launch (start us, length us, event | category | flops | bytes accessed | tf_op | source)
XLA Modules:
  0.0 473.8 jit_solution(18340118177092279685)
XLA Ops:
  7.5 7.1 %collective-permute-start.1 = (bf16[128,256]{1,0:T(8,128)(2,1)S(1)}, bf16[128,256]{1,0:T(8,128)(2,1)S(1)}, u32[]{:S(2)}, u32[]{:S(2)}) collective-permute-start(bf16[128,256]{1,0:T(8,128)(2,1)S(1)} %get-tuple-element.471), channel_id=1, source_target_pairs={{4,0},{8,4},{12,8},{16,12},{20,16},{24,20},{28,24},{32,28},{36,32}... | collective-permute-start | bytes 196616 | tf_op jit(solution)/shard_map/ppermute | solution.py:24
  23.6 4.6 compare_select_fusion.9
  30.1 184.9 %while.55 = (s32[]{:T(128)}, f32[1024,64]{0,1:T(8,128)S(1)}, s32[27,1024]{1,0:T(8,128)}, s32[]{:T(128)}, bf16[1280,256]{1,0:T(8,128)(2,1)S(1)}, /*index=5*/bf16[27,256,64]{1,2,0:T(8,128)(2,1)}, s32[]{:T(128)}, s32[]{:T(128)}) while((s32[]{:T(128)}, f32[1024,64]{0,1:T(8,128)S(1)}, s32[27,1024]{1,0:T(8,128)}, s32[]{:T(128)}, ...), condition=%wide.region_1.2_spmd.clone, body=%wide.region_0.1_spmd.clone.sunk | while | flops 34223104 | bytes 2166903 | solution.py:116
  31.0 3.9 gather_fusion
  37.8 3.9 gather_fusion
  44.6 3.9 gather_fusion
  51.5 3.9 gather_fusion
  58.3 3.9 gather_fusion
  65.2 3.9 gather_fusion
  72.0 3.9 gather_fusion
  78.9 3.9 gather_fusion
  85.7 3.9 gather_fusion
  92.6 3.9 gather_fusion
  99.4 3.9 gather_fusion
  106.3 3.9 gather_fusion
  215.0 13.1 %all_gather.9 = bf16[1024,256]{0,1:T(8,128)(2,1)S(1)} all-gather(bf16[1024,64]{0,1:T(8,128)(2,1)S(1)} %add_convert_fusion.1), channel_id=1, replica_groups=mesh['seg'=64,'ch'=4] {'ch'}, dimensions={1}, use_global_device_ids=true | all-gather | bytes 655360 | tf_op jit(solution)/shard_map/all_gather | solution.py:119
  228.9 9.8 %while.52 = (s32[]{:T(128)}, bf16[2,512,4,16]{1,3,2,0:T(8,128)(2,1)S(1)}, bf16[2,512,4,16]{1,3,2,0:T(8,128)(2,1)S(1)}, bf16[1024,4,16]{0,2,1:T(8,128)(2,1)S(1)}, bf16[1024,4,16]{0,2,1:T(8,128)(2,1)S(1)}, /*index=5*/s32[]{:T(128)}) while((s32[]{:T(128)}, bf16[2,512,4,16]{1,3,2,0:T(8,128)(2,1)S(1)}, bf16[2,512,4,16]{1,3,2,0:T(8,128)(2,1)S(1)}, ...), condition=%wide.region_7.8_spmd, body=%wide.region_4.7_spmd.sunk | while | flops 151056384 | bytes 25600084 | solution.py:80
  240.8 8.6 %gather_fusion.1 = s32[2048]{0:T(1024)S(1)} fusion(s32[1024]{0:T(1024)S(1)} %bitcast.273, s32[2048]{0:T(1024)S(1)} %broadcast_clamp_fusion.4), kind=kCustom, calls=%fused_computation.1 | custom fusion | bytes 24576 | tf_op jit(solution)/shard_map/gather | solution.py:134
  250.9 35.6 %select_select_fusion = s32[2048]{0:T(1024)S(1)} fusion(pred[2048]{0:T(1024)(128)(4,1)S(1)} %get-tuple-element.353, pred[2048]{0:T(1024)(128)(4,1)S(1)} %get-tuple-element.352, pred[2048]{0:T(1024)(128)(4,1)S(1)} %get-tuple-element.351, pred[2048]{0:T(1024)(128)(4,1)S(1)} %get-tuple-element.350, pred[2048]{0:T(1024)(128)(4,1)S(1)} %get-tuple-element.349, ...), kind=kLoop, calls=%fused_computation.243 | loop fusion | flops 116736 | bytes 133348 | tf_op jit(solution)/shard_map/gather | solution.py:142
  286.8 4.5 scatter_custom_fusion
  294.2 5.2 %compare_select_fusion.18 = (s32[1024,1]{0,1:T(1,128)}, s32[1024,1]{0,1:T(1,128)S(1)}) fusion(s32[]{:T(128)} %bitcast.78, s32[]{:T(128)} %bitcast.79, s32[]{:T(128)} %bitcast.80, s32[]{:T(128)} %bitcast.81, s32[]{:T(128)} %bitcast.82, s32[]{:T(128)} %bitcast.84, s32[]{:T(128)} %bitcast.83, s32[1024,1]{0,1:T(1,128)S(1)} %bitcast.296), kind=kLoop, calls=%fused_computation.235 | loop fusion | flops 15360 | bytes 12316 | tf_op jit(solution)/shard_map/gather | solution.py:168
  305.6 7.5 %gather_fusion.2 = bf16[2048,192]{1,0:T(8,128)(2,1)S(1)} fusion(bf16[1024,192]{1,0:T(8,128)(2,1)S(1)} %copy.43, s32[2048]{0:T(1024)S(1)} %broadcast_clamp_fusion.3), kind=kCustom, calls=%fused_computation.2 | custom fusion | bytes 1581056 | tf_op jit(solution)/shard_map/jit(_take)/gather | solution.py:147
  314.4 8.0 %all-to-all-start = ((bf16[64,32,192]{2,1,0:T(8,128)(2,1)}), bf16[64,32,192]{2,1,0:T(8,128)(2,1)S(1)}, u32[]{:S(2)}, u32[]{:S(2)}) async-start(bf16[64,32,192]{2,1,0:T(8,128)(2,1)} %broadcast_select_fusion.1), calls=%async_computation | async-start | bytes 2097152 | tf_op jit(solution)/shard_map/all_to_all | solution.py:150
  323.1 26.2 %all-to-all-done = bf16[64,32,192]{2,1,0:T(8,128)(2,1)S(1)} async-done(((bf16[64,32,192]{2,1,0:T(8,128)(2,1)}), bf16[64,32,192]{2,1,0:T(8,128)(2,1)S(1)}, u32[]{:S(2)}, u32[]{:S(2)}) %all-to-all-start) | async-done | bytes 786464 | tf_op jit(solution)/shard_map/all_to_all | solution.py:150
  349.4 7.5 %gather_fusion.3 = bf16[2048,192]{1,0:T(8,128)(2,1)S(1)} fusion(bf16[2048,192]{1,0:T(8,128)(2,1)S(1)} %bitcast.274, s32[2048]{0:T(1024)S(1)} %broadcast_clamp_fusion.2), kind=kCustom, calls=%fused_computation.3 | custom fusion | bytes 1581056 | tf_op jit(solution)/shard_map/jit(_take)/gather | solution.py:153
  359.3 22.3 %while.54 = (s32[]{:T(128)}, bf16[2,1024,64]{1,2,0:T(8,128)(2,1)S(1)}, bf16[2,1024,3,4,16]{1,4,3,2,0:T(8,128)(2,1)S(1)}, pred[2,1024]{1,0:T(4,128)(4,1)S(1)}, s32[]{:T(128)}, /*index=5*/s32[]{:T(128)}, s32[]{:T(128)}) while((s32[]{:T(128)}, bf16[2,1024,64]{1,2,0:T(8,128)(2,1)S(1)}, bf16[2,1024,3,4,16]{1,4,3,2,0:T(8,128)(2,1)S(1)}, ...), condition=%wide.region_22.23_spmd, body=%wide.region_17.22_spmd.sunk | while | flops 157347840 | bytes 28488956 | solution.py:82
  359.5 10.7 %while.56 = (s32[]{:T(128)}, bf16[2,512,4,16]{1,3,2,0:T(8,128)(2,1)S(1)}, pred[1024]{0:T(1024)(128)(4,1)S(1)}, bf16[2,512,4,16]{1,3,2,0:T(8,128)(2,1)S(1)}, bf16...) while((s32[]{:T(128)}, bf16[2,512,4,16]{1,3,2,0:T(8,128)(2,1)S(1)}, ...), condition=%wide.region_21.21_spmd, body=%wide.region_18.20_spmd.sunk | while | flops 157347840 | bytes 25603164 | solution.py:80
  370.7 10.7 %while.56 = (s32[]{:T(128)}, bf16[2,512,4,16]{1,3,2,0:T(8,128)(2,1)S(1)}, pred[1024]{0:T(1024)(128)(4,1)S(1)}, bf16[2,512,4,16]{1,3,2,0:T(8,128)(2,1)S(1)}, bf16...) while((s32[]{:T(128)}, bf16[2,512,4,16]{1,3,2,0:T(8,128)(2,1)S(1)}, ...), condition=%wide.region_21.21_spmd, body=%wide.region_18.20_spmd.sunk | while | flops 157347840 | bytes 25603164 | solution.py:80
  381.9 6.2 %gather_fusion.4 = bf16[2048,64]{1,0:T(8,128)(2,1)S(1)} fusion(bf16[2048,64]{1,0:T(8,128)(2,1)S(1)} %bitcast.275, s32[2048]{0:T(1024)S(1)} %copy-done.10), kind=kCustom, calls=%fused_computation.4 | custom fusion | bytes 532480 | tf_op jit(solution)/shard_map/jit(_take)/gather | solution.py:158
  389.4 7.8 %all-to-all-start.1 = ((bf16[64,2,1024]{2,1,0:T(2,128)(2,1)}), bf16[64,2,1024]{2,1,0:T(2,128)(2,1)S(1)}, u32[]{:S(2)}, u32[]{:S(2)}) async-start(bf16[64,2,1024]{2,1,0:T(2,128)(2,1)} %reshape.1016), calls=%async_computation.1 | async-start | bytes 524288 | tf_op jit(solution)/shard_map/all_to_all | solution.py:159
  398.4 36.5 %compare_and_fusion.4 = (pred[1024]{0:T(1024)(128)(4,1)S(1)}, s32[1024]{0:T(1024)S(1)}) fusion(s32[1024]{0:T(1024)S(1)} %copy-done.6, pred[1024]{0:T(1024)(128)(4,1)} %get-tuple-element.410, pred[1024]{0:T(1024)(128)(4,1)} %get-tuple-element.409, pred[1024]{0:T(1024)(128)(4,1)} %get-tuple-element.408, pred[1024]{0:T(1024)(128)(4,1)} %get-tuple-element.407, ...), kind=kLoop, calls=%fused_computation.257 | loop fusion | flops 69632 | bytes 76004 | tf_op jit(solution)/shard_map/jit(_take)/and | solution.py:169
  440.5 24.8 %reduce-scatter.2.cloned.1.call-done = bf16[1024,64]{0,1:T(8,128)(2,1)} async-done(((bf16[1024,256]{0,1:T(8,128)(2,1)}), bf16[1024,64]{0,1:T(8,128)(2,1)}) %reduce-scatter.2.cloned.1.call-update) | async-done | bytes 131088 | tf_op jit(solution)/shard_map/reduce_scatter | solution.py:172
  (374 shorter events, 207.0 us)
Async XLA Ops:
  6.5 232.4 %copy-start = (bf16[256,256]{1,0:T(8,128)(2,1)S(1)}, bf16[256,256]{1,0:T(8,128)(2,1)}, u32[]{:S(2)}) copy-start(bf16[256,256]{1,0:T(8,128)(2,1)} %param.23) | copy-start | bytes 393220
  6.5 295.1 %all-gather.3.cloned.1.call-start = ((), (), s32[]{:S(2)}) async-start(), calls=%async_computation.4 | async-start | bytes 2621440 | tf_op jit(solution)/shard_map/all_gather | solution.py:125
  7.5 21.5 %collective-permute-start.1 = (bf16[128,256]{1,0:T(8,128)(2,1)S(1)}, bf16[128,256]{1,0:T(8,128)(2,1)S(1)}, u32[]{:S(2)}, u32[]{:S(2)}) collective-permute-start(bf16[128,256]{1,0:T(8,128)(2,1)S(1)} %get-tuple-element.471), channel_id=1, source_target_pairs={{4,0},{8,4},{12,8},{16,12},{20,16},{24,20},{28,24},{32,28},{36,32}... | collective-permute-start | bytes 196616 | tf_op jit(solution)/shard_map/ppermute | solution.py:24
  14.6 14.4 %collective-permute-start = (bf16[128,256]{1,0:T(8,128)(2,1)S(1)}, bf16[128,256]{1,0:T(8,128)(2,1)S(1)}, u32[]{:S(2)}, u32[]{:S(2)}) collective-permute-start(bf16[128,256]{1,0:T(8,128)(2,1)S(1)} %get-tuple-element.470), channel_id=1, source_target_pairs={{0,4},{4,8},{8,12},{12,16},{16,20},{20,24},{24,28},{28,32},{32,36}... | collective-permute-start | bytes 196616 | tf_op jit(solution)/shard_map/ppermute | solution.py:22
  23.4 269.9 %copy-start.3 = (s32[64]{0:T(128)}, s32[64]{0:T(128)S(1)}, u32[]{:S(2)}) copy-start(s32[64]{0:T(128)S(1)} %bitcast_subtract_fusion) | copy-start | bytes 772
  30.1 198.3 %copy-start.46 = (bf16[256,3,64]{0,2,1:T(8,128)(2,1)S(1)}, bf16[256,3,64]{0,2,1:T(8,128)(2,1)}, u32[]{:S(2)}) copy-start(bf16[256,3,64]{0,2,1:T(8,128)(2,1)} %param.22) | copy-start | bytes 294916
  240.8 64.3 %copy-start.47 = (bf16[256,3,64]{0,2,1:T(8,128)(2,1)S(1)}, bf16[256,3,64]{0,2,1:T(8,128)(2,1)}, u32[]{:S(2)}) copy-start(bf16[256,3,64]{0,2,1:T(8,128)(2,1)} %param.24) | copy-start | bytes 294916
  314.4 35.0 %all-to-all-start = ((bf16[64,32,192]{2,1,0:T(8,128)(2,1)}), bf16[64,32,192]{2,1,0:T(8,128)(2,1)S(1)}, u32[]{:S(2)}, u32[]{:S(2)}) async-start(bf16[64,32,192]{2,1,0:T(8,128)(2,1)} %broadcast_select_fusion.1), calls=%async_computation | async-start | bytes 2097152 | tf_op jit(solution)/shard_map/all_to_all | solution.py:150
  358.9 39.1 %copy-start.6 = (s32[1024]{0:T(1024)S(1)}, s32[1024]{0:T(1024)}, u32[]{:S(2)}) copy-start(s32[1024]{0:T(1024)} %copy-done.5) | copy-start | bytes 12292
  358.9 39.1 %copy-start.8 = (s32[1024]{0:T(1024)S(1)}, s32[1024]{0:T(1024)}, u32[]{:S(2)}) copy-start(s32[1024]{0:T(1024)} %copy-done.7) | copy-start | bytes 12292
  358.9 39.1 %copy-start.11 = (s32[1024,1]{0,1:T(1,128)S(1)}, s32[1024,1]{0,1:T(1,128)}, u32[]{:S(2)}) copy-start(s32[1024,1]{0,1:T(1,128)} %get-tuple-element.457) | copy-start | bytes 12292
  358.9 39.1 %copy-start.12 = (pred[1024]{0:T(1024)(128)(4,1)S(1)}, pred[1024]{0:T(1024)(128)(4,1)}, u32[]{:S(2)}) copy-start(pred[1024]{0:T(1024)(128)(4,1)} %get-tuple-element.354) | copy-start | bytes 3076
  358.9 39.1 %copy-start.13 = (pred[1024]{0:T(1024)(128)(4,1)S(1)}, pred[1024]{0:T(1024)(128)(4,1)}, u32[]{:S(2)}) copy-start(pred[1024]{0:T(1024)(128)(4,1)} %get-tuple-element.355) | copy-start | bytes 3076
  359.0 39.1 %copy-start.14 = (pred[1024]{0:T(1024)(128)(4,1)S(1)}, pred[1024]{0:T(1024)(128)(4,1)}, u32[]{:S(2)}) copy-start(pred[1024]{0:T(1024)(128)(4,1)} %get-tuple-element.356) | copy-start | bytes 3076
  359.0 39.1 %copy-start.15 = (pred[1024]{0:T(1024)(128)(4,1)S(1)}, pred[1024]{0:T(1024)(128)(4,1)}, u32[]{:S(2)}) copy-start(pred[1024]{0:T(1024)(128)(4,1)} %get-tuple-element.357) | copy-start | bytes 3076
  359.0 39.1 %copy-start.16 = (pred[1024]{0:T(1024)(128)(4,1)S(1)}, pred[1024]{0:T(1024)(128)(4,1)}, u32[]{:S(2)}) copy-start(pred[1024]{0:T(1024)(128)(4,1)} %get-tuple-element.358) | copy-start | bytes 3076
  359.0 39.1 %copy-start.17 = (pred[1024]{0:T(1024)(128)(4,1)S(1)}, pred[1024]{0:T(1024)(128)(4,1)}, u32[]{:S(2)}) copy-start(pred[1024]{0:T(1024)(128)(4,1)} %get-tuple-element.359) | copy-start | bytes 3076
  359.0 39.1 %copy-start.18 = (pred[1024]{0:T(1024)(128)(4,1)S(1)}, pred[1024]{0:T(1024)(128)(4,1)}, u32[]{:S(2)}) copy-start(pred[1024]{0:T(1024)(128)(4,1)} %get-tuple-element.360) | copy-start | bytes 3076
  359.0 39.1 %copy-start.19 = (pred[1024]{0:T(1024)(128)(4,1)S(1)}, pred[1024]{0:T(1024)(128)(4,1)}, u32[]{:S(2)}) copy-start(pred[1024]{0:T(1024)(128)(4,1)} %get-tuple-element.361) | copy-start | bytes 3076
  359.0 39.1 %copy-start.20 = (pred[1024]{0:T(1024)(128)(4,1)S(1)}, pred[1024]{0:T(1024)(128)(4,1)}, u32[]{:S(2)}) copy-start(pred[1024]{0:T(1024)(128)(4,1)} %get-tuple-element.362) | copy-start | bytes 3076
  359.0 39.1 %copy-start.21 = (pred[1024]{0:T(1024)(128)(4,1)S(1)}, pred[1024]{0:T(1024)(128)(4,1)}, u32[]{:S(2)}) copy-start(pred[1024]{0:T(1024)(128)(4,1)} %get-tuple-element.363) | copy-start | bytes 3076
  359.0 39.1 %copy-start.22 = (pred[1024]{0:T(1024)(128)(4,1)S(1)}, pred[1024]{0:T(1024)(128)(4,1)}, u32[]{:S(2)}) copy-start(pred[1024]{0:T(1024)(128)(4,1)} %get-tuple-element.364) | copy-start | bytes 3076
  359.0 39.1 %copy-start.23 = (pred[1024]{0:T(1024)(128)(4,1)S(1)}, pred[1024]{0:T(1024)(128)(4,1)}, u32[]{:S(2)}) copy-start(pred[1024]{0:T(1024)(128)(4,1)} %get-tuple-element.365) | copy-start | bytes 3076
  359.1 39.1 %copy-start.24 = (pred[1024]{0:T(1024)(128)(4,1)S(1)}, pred[1024]{0:T(1024)(128)(4,1)}, u32[]{:S(2)}) copy-start(pred[1024]{0:T(1024)(128)(4,1)} %get-tuple-element.366) | copy-start | bytes 3076
  359.1 39.1 %copy-start.25 = (pred[1024]{0:T(1024)(128)(4,1)S(1)}, pred[1024]{0:T(1024)(128)(4,1)}, u32[]{:S(2)}) copy-start(pred[1024]{0:T(1024)(128)(4,1)} %get-tuple-element.367) | copy-start | bytes 3076
  359.1 39.1 %copy-start.26 = (pred[1024]{0:T(1024)(128)(4,1)S(1)}, pred[1024]{0:T(1024)(128)(4,1)}, u32[]{:S(2)}) copy-start(pred[1024]{0:T(1024)(128)(4,1)} %get-tuple-element.368) | copy-start | bytes 3076
  359.1 39.1 %copy-start.27 = (pred[1024]{0:T(1024)(128)(4,1)S(1)}, pred[1024]{0:T(1024)(128)(4,1)}, u32[]{:S(2)}) copy-start(pred[1024]{0:T(1024)(128)(4,1)} %get-tuple-element.369) | copy-start | bytes 3076
  359.1 39.1 %copy-start.28 = (pred[1024]{0:T(1024)(128)(4,1)S(1)}, pred[1024]{0:T(1024)(128)(4,1)}, u32[]{:S(2)}) copy-start(pred[1024]{0:T(1024)(128)(4,1)} %get-tuple-element.370) | copy-start | bytes 3076
  359.1 39.1 %copy-start.29 = (pred[1024]{0:T(1024)(128)(4,1)S(1)}, pred[1024]{0:T(1024)(128)(4,1)}, u32[]{:S(2)}) copy-start(pred[1024]{0:T(1024)(128)(4,1)} %get-tuple-element.371) | copy-start | bytes 3076
  359.1 39.1 %copy-start.30 = (pred[1024]{0:T(1024)(128)(4,1)S(1)}, pred[1024]{0:T(1024)(128)(4,1)}, u32[]{:S(2)}) copy-start(pred[1024]{0:T(1024)(128)(4,1)} %get-tuple-element.372) | copy-start | bytes 3076
  389.4 45.5 %all-to-all-start.1 = ((bf16[64,2,1024]{2,1,0:T(2,128)(2,1)}), bf16[64,2,1024]{2,1,0:T(2,128)(2,1)S(1)}, u32[]{:S(2)}, u32[]{:S(2)}) async-start(bf16[64,2,1024]{2,1,0:T(2,128)(2,1)} %reshape.1016), calls=%async_computation.1 | async-start | bytes 524288 | tf_op jit(solution)/shard_map/all_to_all | solution.py:159
  397.2 68.1 %reduce-scatter.2.cloned.1.call-start = ((), (), s32[]{:S(2)}) async-start(), calls=%async_computation.3 | async-start | bytes 655360 | tf_op jit(solution)/shard_map/reduce_scatter | solution.py:172
  (22 other events, 711.9 us)
Sparse Core Ops, SparseCore 0:
  240.2 31.4 all-gather.2
  440.7 24.6 reduce-scatter.1
